TPU v7x, 128 devices: a whole 4x4x4 slice. The times are simulated.
128 devices in a mesh: ctx: 16 (over z, y_hi, core), tp: 8 (over y_lo, x).
Axes of the slice: x: 4, y: 4 (y_hi: 2, y_lo: 2; y = y_hi * 2 + y_lo), z: 4, core: 2. Of those that a mesh axis runs over, the one named last changes fastest.
Arguments:
- trunk_out: bfloat16 [8192, 1536], P('ctx', 'tp'), may hold values from -6 to 6
- proj_weight: bfloat16 [1536, 384], replicated, may hold values from -0.15625 to 0.15625
- base_skip: bfloat16 [1048576, 384], P(('ctx', 'tp')), may hold values from -6 to 6
- conv_weight: bfloat16 [2, 3, 384, 384], replicated, may hold values from -0.1875 to 0.1875
- head_hidden: bfloat16 [56, 384, 768], P('tp'), may hold values from -0.3125 to 0.3125
- head_logit: bfloat16 [56, 768], P('tp'), may hold values from -0.21875 to 0.21875
- site_index: int32 [16384], P(('ctx', 'tp')), may hold values from 0 to 8191
- tissue_slot: int32 [54], replicated, may hold values from 0 to 55, as said below
Outputs:
- usage: float32 [54, 16384], P(None, ('ctx', 'tp'))
- tower: bfloat16 [1048576, 384], P(('ctx', 'tp'))
Inputs may be any that keep to these rules, and one draw needn't show every extreme that they name: tissue_slot holds 54 different slots of the 56 slots.
All inputs are finite; a program needn't handle non-finite values.
Results may differ from a plain program's by a relative error of at most 0.02.
Values may be sent and summed in bfloat16 or wider, within the bound.
A program may use at most 320 MiB of HBM per device.

v0:
```python
import functools

import jax
import jax.numpy as jnp
from jax import lax
from jax.experimental import pallas as pl
from jax.experimental.pallas import tpu as pltpu
from jax.sharding import PartitionSpec as P

BASES = 128
EPSILON = 1e-06
MESH = pl.DeviceIdType.MESH
BF16 = jnp.bfloat16
F32 = jnp.float32


def normalize(values):
    wide = values.astype(F32)
    mean = jnp.sum(wide * wide, axis=-1, keepdims=True) * (1.0 / values.shape[-1])
    return (wide * lax.rsqrt(mean + EPSILON)).astype(BF16)


def gelu(x):
    inner = x * (0.7978845608028654 + 0.035677408136300125 * (x * x))
    half = 0.5 * x
    return half + half * jnp.tanh(inner)


def kernel(
    dims,
    trunk, projw, base, convw, headw, headl, site, tissue,
    usage, tower,
    cur, n1, n2, raw, trunk_all, proj, pw, cw, hw, wl, sites, picked, chosen, logit_out, logit_in,
    local_sem, trunk_send, trunk_recv, raw_send, raw_recv, proj_send, proj_recv,
    halo_send, halo_recv, tower_sem, chosen_send, chosen_recv, logit_send, logit_recv,
):
    n_ctx, n_tp, tile, channels, near, far, chunk = dims
    count = far // chunk
    tokens = tile // BASES
    near_tokens = near // BASES
    cands = site.shape[1]
    slots = headl.shape[0]
    ctx = lax.axis_index("ctx")
    tp = lax.axis_index("tp")
    place = ctx * n_tp + tp
    total = n_ctx * n_tp
    left_at = lax.rem(place + total - 1, total)
    right_at = lax.rem(place + 1, total)
    left = {"ctx": left_at // n_tp, "tp": lax.rem(left_at, n_tp)}
    right = {"ctx": right_at // n_tp, "tp": lax.rem(right_at, n_tp)}
    first_tile = place == 0
    last_tile = place == total - 1

    def peer(step):
        return lax.rem(tp + step, n_tp)

    def remote(src, dst, send, recv, device):
        return pltpu.make_async_remote_copy(
            src_ref=src, dst_ref=dst, send_sem=send, recv_sem=recv,
            device_id=device, device_id_type=MESH,
        )

    loads = [
        pltpu.make_async_copy(projw, pw, local_sem.at[0]),
        pltpu.make_async_copy(base, cur, local_sem.at[1]),
        pltpu.make_async_copy(convw, cw, local_sem.at[2]),
        pltpu.make_async_copy(headw, hw, local_sem.at[3]),
        pltpu.make_async_copy(
            trunk.at[pl.ds(tp * tokens, tokens)], trunk_all.at[tp], local_sem.at[4]
        ),
    ]
    loads[4].start()
    for load in loads[:4]:
        load.start()

    barrier = pltpu.get_barrier_semaphore()
    for device in (left, right):
        pl.semaphore_signal(barrier, inc=1, device_id=device, device_id_type=MESH)
    for step in range(1, n_tp):
        pl.semaphore_signal(
            barrier, inc=1, device_id={"ctx": ctx, "tp": peer(step)}, device_id_type=MESH
        )
    pl.semaphore_wait(barrier, n_tp + 1)

    trunk_copies = []
    for step in range(1, n_tp):
        to = peer(step)
        copy = remote(
            trunk.at[pl.ds(to * tokens, tokens)], trunk_all.at[tp],
            trunk_send.at[step - 1], trunk_recv.at[step - 1], {"ctx": ctx, "tp": to},
        )
        copy.start()
        trunk_copies.append(copy)
    raw_copies = [
        remote(base.at[pl.ds(tile - near, near)], raw.at[0], raw_send.at[0], raw_recv.at[0], right),
        remote(base.at[pl.ds(0, near)], raw.at[1], raw_send.at[1], raw_recv.at[1], left),
    ]
    for copy in raw_copies:
        copy.start()

    sites[...] = jnp.broadcast_to(site[...], (cands, cands)).T
    wl[...] = jnp.zeros_like(wl)
    wl[pl.ds(0, slots), :] = headl[...].astype(F32)
    picked[...] = jnp.zeros_like(picked)

    loads[4].wait()
    loads[0].wait()
    total_proj = jnp.dot(trunk_all[tp], pw[tp], preferred_element_type=F32)
    for step in range(1, n_tp):
        trunk_copies[step - 1].wait_recv()
        source = lax.rem(tp + n_tp - step, n_tp)
        total_proj += jnp.dot(trunk_all[source], pw[source], preferred_element_type=F32)
    proj[pl.ds(near_tokens, tokens), :] = total_proj
    loads[1].wait()

    def add_token(token, rows, at_proj):
        lifted = rows.astype(F32) + proj[pl.ds(at_proj, 1), :]
        return lifted.astype(BF16)

    def own_rows(step, carry):
        for part in range(2):
            token = step * 2 + part
            at = pl.multiple_of(token * BASES, BASES)
            value = add_token(token, cur[pl.ds(at, BASES), :], token + near_tokens)
            cur[pl.ds(at, BASES), :] = value
            n1[pl.ds(at + near, BASES), :] = normalize(value)
        return carry

    lax.fori_loop(0, tokens // 4, own_rows, 0)
    proj_copies = [
        remote(
            proj.at[pl.ds(tokens, near_tokens)], proj.at[pl.ds(0, near_tokens)],
            proj_send.at[0], proj_recv.at[0], right,
        ),
        remote(
            proj.at[pl.ds(near_tokens, near_tokens)],
            proj.at[pl.ds(tokens + near_tokens, near_tokens)],
            proj_send.at[1], proj_recv.at[1], left,
        ),
    ]
    for copy in proj_copies:
        copy.start()
    lax.fori_loop(tokens // 4, tokens // 2, own_rows, 0)
    loads[2].wait()

    def pair_of(ref, at):
        return jnp.concatenate(
            [
                ref[pl.ds(pl.multiple_of(at, chunk), chunk), :],
                ref[pl.ds(pl.multiple_of(at + far, chunk), chunk), :],
            ],
            axis=0,
        )

    def chunk_of(step):
        return lax.rem(step + near // chunk, count)

    def halo_copy(index, side):
        at = pl.multiple_of(index * chunk, chunk)
        if side == 0:
            return remote(
                n2.at[pl.ds(at + 2 * far, chunk)], n2.at[pl.ds(at, chunk)],
                halo_send.at[0, index], halo_recv.at[0, index], right,
            )
        return remote(
            n2.at[pl.ds(at + far, chunk)], n2.at[pl.ds(at + 3 * far, chunk)],
            halo_send.at[1, index], halo_recv.at[1, index], left,
        )

    def send_chunk(step):
        index = chunk_of(step)
        halo_copy(index, 0).start()
        halo_copy(index, 1).start()

    def block_one(step, carry):
        at = pl.multiple_of(chunk_of(step) * chunk, chunk)
        window = jnp.concatenate(
            [pair_of(n1, at), pair_of(n1, at + near), pair_of(n1, at + 2 * near)], axis=1
        )
        mixed = jnp.dot(window, cw[0], preferred_element_type=F32)
        value = (pair_of(cur, at).astype(F32) + gelu(mixed)).astype(BF16)
        scaled = normalize(value)
        for part in range(2):
            rows = slice(part * chunk, (part + 1) * chunk)
            cur[pl.ds(at + part * far, chunk), :] = value[rows]
            n2[pl.ds(at + (part + 1) * far, chunk), :] = scaled[rows]

        @pl.when(step > 0)
        def _():
            send_chunk(step - 1)

        return carry

    middle = (far - near) // chunk - near // chunk
    lax.fori_loop(0, middle, block_one, 0)

    for copy in raw_copies:
        copy.wait_recv()
    for copy in proj_copies:
        copy.wait_recv()

    def halo_rows(step, carry):
        at = pl.multiple_of(step * BASES, BASES)
        low = normalize(add_token(step, raw[0, pl.ds(at, BASES), :], step))
        n1[pl.ds(at, BASES), :] = jnp.where(first_tile, jnp.zeros_like(low), low)
        high = normalize(
            add_token(step, raw[1, pl.ds(at, BASES), :], step + tokens + near_tokens)
        )
        n1[pl.ds(at + tile + near, BASES), :] = jnp.where(last_tile, jnp.zeros_like(high), high)
        return carry

    lax.fori_loop(0, near_tokens, halo_rows, 0)
    lax.fori_loop(middle, count, block_one, 0)
    send_chunk(count - 1)

    lane = lax.broadcasted_iota(jnp.int32, (cands, chunk), 1)
    site_wide = jnp.concatenate([sites[...]] * (chunk // cands), axis=1)

    def tower_copy(index, part):
        rows = pl.ds(pl.multiple_of(index * chunk + part * far, chunk), chunk)
        return pltpu.make_async_copy(cur.at[rows], tower.at[rows], tower_sem.at[part, index])

    def block_two(step, carry):
        index = chunk_of(step)
        at = pl.multiple_of(index * chunk, chunk)
        halo_copy(index, 0).wait_recv()
        halo_copy(index, 1).wait_recv()
        low = n2[pl.ds(at, chunk), :]
        low = jnp.where(first_tile, jnp.zeros_like(low), low)
        one = n2[pl.ds(at + far, chunk), :]
        two = n2[pl.ds(at + 2 * far, chunk), :]
        high = n2[pl.ds(at + 3 * far, chunk), :]
        high = jnp.where(last_tile, jnp.zeros_like(high), high)
        window = jnp.concatenate(
            [
                jnp.concatenate([low, one], axis=0),
                jnp.concatenate([one, two], axis=0),
                jnp.concatenate([two, high], axis=0),
            ],
            axis=1,
        )
        mixed = jnp.dot(window, cw[1], preferred_element_type=F32)
        value = (pair_of(cur, at).astype(F32) + gelu(mixed)).astype(BF16)
        for part in range(2):
            cur[pl.ds(at + part * far, chunk), :] = value[part * chunk:(part + 1) * chunk]
        hits = jnp.concatenate(
            [
                jnp.where(site_wide == lane + (at + part * far), 1.0, 0.0).astype(BF16)
                for part in range(2)
            ],
            axis=1,
        )
        picked[...] += jnp.dot(hits, value, preferred_element_type=F32)
        for part in range(2):
            tower_copy(index, part).start()
        return carry

    lax.fori_loop(0, count, block_two, 0)
    loads[3].wait()
    chosen[tp] = normalize(picked[...])

    def drain(index, carry):
        for side in range(2):
            halo_copy(index, side).wait_send()
        return carry

    lax.fori_loop(0, count, drain, 0)

    def chosen_copy(step):
        return remote(
            chosen.at[tp], chosen.at[tp], chosen_send.at[step - 1], chosen_recv.at[step - 1],
            {"ctx": ctx, "tp": peer(step)},
        )

    for step in range(1, n_tp):
        chosen_copy(step).start()

    def logit_copy(to):
        step = lax.rem(to + n_tp - tp, n_tp)
        return remote(
            logit_out.at[pl.ds(pl.multiple_of(to * 8, 8), 8)],
            logit_in.at[pl.ds(pl.multiple_of(tp * 8, 8), 8)],
            logit_send.at[step - 1], logit_recv.at[step - 1], {"ctx": ctx, "tp": to},
        )

    row = lax.broadcasted_iota(jnp.int32, wl.shape, 0)

    def heads(step, carry):
        pair = lax.rem(tp // 2 + step, n_tp // 2)
        for part in range(2):
            source = pair * 2 + part

            @pl.when(source != tp)
            def _():
                away = lax.rem(tp + n_tp - source, n_tp)
                remote(
                    chosen.at[source], chosen.at[source],
                    chosen_send.at[away - 1], chosen_recv.at[away - 1], {"ctx": ctx, "tp": source},
                ).wait_recv()

        rows_in = jnp.concatenate([chosen[pair * 2], chosen[pair * 2 + 1]], axis=0)
        scores = jnp.zeros((8, 2 * cands), F32)
        for slot in range(slots):
            hidden = gelu(jnp.dot(rows_in, hw[slot], preferred_element_type=F32)).astype(BF16)
            weights = jnp.where(row == slot, wl[...], 0.0).astype(BF16)
            scores += lax.dot_general(
                weights, hidden, (((1,), (1,)), ((), ())), preferred_element_type=F32
            )
        for part in range(2):
            source = pair * 2 + part
            logit_out[pl.ds(pl.multiple_of(source * 8, 8), 8), :] = (
                scores[:, part * cands:(part + 1) * cands]
            )
        for part in range(2):
            source = pair * 2 + part

            @pl.when(source != tp)
            def _():
                logit_copy(source).start()

        return carry

    lax.fori_loop(0, n_tp // 2, heads, 0)
    own = pl.ds(pl.multiple_of(tp * 8, 8), 8)
    logit_in[own, :] = logit_out[own, :]
    for step in range(1, n_tp):
        chosen_copy(step).wait_send()
        trunk_copies[step - 1].wait_send()
    for copy in raw_copies + proj_copies:
        copy.wait_send()

    def drain_tower(index, carry):
        for part in range(2):
            tower_copy(index, part).wait()
        return carry

    lax.fori_loop(0, count, drain_tower, 0)
    for step in range(1, n_tp):
        copy = logit_copy(peer(step))
        copy.wait_send()
        copy.wait_recv()
    for tissue_at in range(usage.shape[0]):
        slot = tissue[tissue_at]
        at = (slot // slots) * 8 + lax.rem(slot, slots)
        usage[pl.ds(tissue_at, 1), :] = logit_in[pl.ds(at, 1), :]


def on_device(
    n_ctx, n_tp,
    trunk_out, proj_weight, base_skip, conv_weight, head_hidden, head_logit, site_index, tissue_slot,
):
    tile, channels = base_skip.shape
    width = proj_weight.shape[0]
    near, far, chunk = tile // 8, tile // 2, 256
    count = far // chunk
    tokens = tile // BASES
    near_tokens = near // BASES
    cands = site_index.shape[0]
    slots, _, hidden = head_hidden.shape
    tissues = tissue_slot.shape[0]
    share = width // n_tp
    dims = (n_ctx, n_tp, tile, channels, near, far, chunk)
    anywhere = pl.BlockSpec(memory_space=pl.ANY)
    vmem = pl.BlockSpec(memory_space=pltpu.VMEM)
    smem = pl.BlockSpec(memory_space=pltpu.SMEM)
    dma = pltpu.SemaphoreType.DMA
    usage, tower = pl.pallas_call(
        functools.partial(kernel, dims),
        out_shape=(
            jax.ShapeDtypeStruct((tissues, cands), F32),
            jax.ShapeDtypeStruct((tile, channels), BF16),
        ),
        in_specs=[anywhere] * 5 + [vmem, vmem, smem],
        out_specs=(vmem, anywhere),
        scratch_shapes=[
            pltpu.VMEM((tile, channels), BF16),
            pltpu.VMEM((tile + 2 * near, channels), BF16),
            pltpu.VMEM((tile + 2 * far, channels), BF16),
            pltpu.VMEM((2, near, channels), BF16),
            pltpu.VMEM((n_tp, tokens, share), BF16),
            pltpu.VMEM((tokens + 2 * near_tokens, channels), F32),
            pltpu.VMEM((n_tp, share, channels), BF16),
            pltpu.VMEM((2, 3 * channels, channels), BF16),
            pltpu.VMEM((slots, channels, hidden), BF16),
            pltpu.VMEM((8, hidden), F32),
            pltpu.VMEM((cands, cands), jnp.int32),
            pltpu.VMEM((cands, channels), F32),
            pltpu.VMEM((n_tp, cands, channels), BF16),
            pltpu.VMEM((n_tp * 8, cands), F32),
            pltpu.VMEM((n_tp * 8, cands), F32),
            dma((5,)), dma((n_tp - 1,)), dma((n_tp - 1,)), dma((2,)), dma((2,)), dma((2,)), dma((2,)),
            dma((2, count)), dma((2, count)), dma((2, count)),
            dma((n_tp - 1,)), dma((n_tp - 1,)), dma((n_tp - 1,)), dma((n_tp - 1,)),
        ],
        compiler_params=pltpu.CompilerParams(
            collective_id=0, has_side_effects=True, vmem_limit_bytes=60 * 1024 * 1024
        ),
    )(
        trunk_out,
        proj_weight.reshape(n_tp, share, channels),
        base_skip,
        conv_weight.reshape(2, 3 * channels, channels),
        head_hidden,
        head_logit,
        site_index.reshape(1, cands),
        tissue_slot,
    )
    return usage, tower


def solution(mesh):
    return jax.shard_map(
        functools.partial(on_device, mesh.shape["ctx"], mesh.shape["tp"]),
        mesh=mesh,
        in_specs=(
            P("ctx", "tp"),
            P(),
            P(("ctx", "tp"), None),
            P(),
            P("tp", None, None),
            P("tp", None),
            P(("ctx", "tp")),
            P(),
        ),
        out_specs=(P(None, ("ctx", "tp")), P(("ctx", "tp"), None)),
        check_vma=False,
    )
```

profile of v0, /device:TPU:0, one launch (start us, length us, event | category | flops | bytes accessed | tf_op | source)
XLA Modules:
  0.0 160.7 jit_solution(6740138632009304448)
XLA Ops:
  0.6 1.8 %copy.10.trunk = bf16[512,192]{1,0:T(8,128)(2,1)} copy(bf16[512,192]{0,1:T(8,128)(2,1)} %param.8) | data formatting | bytes 393216 | tf_op args[0]
  2.4 150.8 %shard_map.95 = (f32[54,128]{1,0:T(8,128)}, bf16[8192,384]{1,0:T(8,128)(2,1)}) custom-call(bf16[512,192]{1,0:T(8,128)(2,1)} %copy.10.trunk, bf16[8,192,384]{2,1,0:T(8,128)(2,1)} %bitcast.4, bf16[8192,384]{1,0:T(8,128)(2,1)} %base.1, bf16[2,1152,384]{2,1,0:T(8,128)(2,1)} %bitcast.3, bf16[7,384,768]{2,1,0:T(8,128)(2,1)} %headw.1, bf16[7,768]{1,0:T(8,128)(2,1)} %headl.1, ...), custom_call_target="tpu_custom_call" | custom-call | tf_op jit(solution)/shard_map/pallas_call | solution.py:367
  153.2 1.4 copy.13
  154.6 6.1 %copy.14 = bf16[8192,384]{1,0:T(8,128)(2,1)} copy(bf16[8192,384]{1,0:T(8,128)(2,1)} %get-tuple-element.5) | data formatting | bytes 12582912
where the time goes:
time: 161 us
  Pallas kernels  151 us (94%)
  local copies, waits for them, and re-layouts  9.24 us (6%)
    pallas_call x1, Pallas kernels, on_device(): pl.pallas_call(functools.partial(kernel, dims), out_shape=(jax.ShapeDtype...  151 us
    unnamed x3, local copies, waits for them, and re-layouts  9.24 us

commit v1 on v0

--- a/solution.py
+++ b/solution.py
@@ -95,8 +95,11 @@
         remote(base.at[pl.ds(tile - near, near)], raw.at[0], raw_send.at[0], raw_recv.at[0], right),
         remote(base.at[pl.ds(0, near)], raw.at[1], raw_send.at[1], raw_recv.at[1], left),
     ]
-    for copy in raw_copies:
-        copy.start()
+    def both(low, high):
+        pl.when(jnp.logical_not(first_tile))(low)
+        pl.when(jnp.logical_not(last_tile))(high)
+
+    both(raw_copies[1].start, raw_copies[0].start)
 
     sites[...] = jnp.broadcast_to(site[...], (cands, cands)).T
     wl[...] = jnp.zeros_like(wl)
@@ -138,8 +141,7 @@
             proj_send.at[1], proj_recv.at[1], left,
         ),
     ]
-    for copy in proj_copies:
-        copy.start()
+    both(proj_copies[1].start, proj_copies[0].start)
     lax.fori_loop(tokens // 4, tokens // 2, own_rows, 0)
     loads[2].wait()
 
@@ -169,8 +171,7 @@
 
     def send_chunk(step):
         index = chunk_of(step)
-        halo_copy(index, 0).start()
-        halo_copy(index, 1).start()
+        both(halo_copy(index, 1).start, halo_copy(index, 0).start)
 
     def block_one(step, carry):
         at = pl.multiple_of(chunk_of(step) * chunk, chunk)
@@ -194,22 +195,29 @@
     middle = (far - near) // chunk - near // chunk
     lax.fori_loop(0, middle, block_one, 0)
 
-    for copy in raw_copies:
-        copy.wait_recv()
-    for copy in proj_copies:
-        copy.wait_recv()
-
-    def halo_rows(step, carry):
-        at = pl.multiple_of(step * BASES, BASES)
-        low = normalize(add_token(step, raw[0, pl.ds(at, BASES), :], step))
-        n1[pl.ds(at, BASES), :] = jnp.where(first_tile, jnp.zeros_like(low), low)
-        high = normalize(
-            add_token(step, raw[1, pl.ds(at, BASES), :], step + tokens + near_tokens)
-        )
-        n1[pl.ds(at + tile + near, BASES), :] = jnp.where(last_tile, jnp.zeros_like(high), high)
-        return carry
-
-    lax.fori_loop(0, near_tokens, halo_rows, 0)
+    for side, edge in ((0, first_tile), (1, last_tile)):
+        start = side * (tile + near)
+
+        @pl.when(edge)
+        def _():
+            n1[pl.ds(start, near), :] = jnp.zeros((near, channels), BF16)
+            n2[pl.ds(side * 3 * far, far), :] = jnp.zeros((far, channels), BF16)
+
+        @pl.when(jnp.logical_not(edge))
+        def _():
+            raw_copies[side].wait_recv()
+            proj_copies[side].wait_recv()
+
+            def halo_rows(step, carry):
+                at = pl.multiple_of(step * BASES, BASES)
+                token = step + side * (tokens + near_tokens)
+                n1[pl.ds(at + start, BASES), :] = normalize(
+                    add_token(token, raw[side, pl.ds(at, BASES), :], token)
+                )
+                return carry
+
+            lax.fori_loop(0, near_tokens, halo_rows, 0)
+
     lax.fori_loop(middle, count, block_one, 0)
     send_chunk(count - 1)
 
@@ -223,14 +231,11 @@
     def block_two(step, carry):
         index = chunk_of(step)
         at = pl.multiple_of(index * chunk, chunk)
-        halo_copy(index, 0).wait_recv()
-        halo_copy(index, 1).wait_recv()
+        both(halo_copy(index, 0).wait_recv, halo_copy(index, 1).wait_recv)
         low = n2[pl.ds(at, chunk), :]
-        low = jnp.where(first_tile, jnp.zeros_like(low), low)
         one = n2[pl.ds(at + far, chunk), :]
         two = n2[pl.ds(at + 2 * far, chunk), :]
         high = n2[pl.ds(at + 3 * far, chunk), :]
-        high = jnp.where(last_tile, jnp.zeros_like(high), high)
         window = jnp.concatenate(
             [
                 jnp.concatenate([low, one], axis=0),
@@ -260,8 +265,7 @@
     chosen[tp] = normalize(picked[...])
 
     def drain(index, carry):
-        for side in range(2):
-            halo_copy(index, side).wait_send()
+        both(halo_copy(index, 1).wait_send, halo_copy(index, 0).wait_send)
         return carry
 
     lax.fori_loop(0, count, drain, 0)
@@ -326,8 +330,8 @@
     for step in range(1, n_tp):
         chosen_copy(step).wait_send()
         trunk_copies[step - 1].wait_send()
-    for copy in raw_copies + proj_copies:
-        copy.wait_send()
+    for copies in (raw_copies, proj_copies):
+        both(copies[1].wait_send, copies[0].wait_send)
 
     def drain_tower(index, carry):
         for part in range(2):

time: 161 us -> 161 us (level)
  no operation moved by 1% of the time
where the time goes in v1:
time: 161 us
  Pallas kernels  151 us (94%)
  local copies, waits for them, and re-layouts  9.24 us (6%)
    pallas_call x1, Pallas kernels, on_device(): pl.pallas_call(functools.partial(kernel, dims), out_shape=(jax.ShapeDtype...  151 us
    unnamed x3, local copies, waits for them, and re-layouts  9.24 us

profile of v1, /device:TPU:0, one launch (start us, length us, event | category | flops | bytes accessed | tf_op | source)
XLA Modules:
  0.0 160.7 jit_solution(14862570713894000492)
XLA Ops:
  0.6 1.8 %copy.10.trunk = bf16[512,192]{1,0:T(8,128)(2,1)} copy(bf16[512,192]{0,1:T(8,128)(2,1)} %param.8) | data formatting | bytes 393216 | tf_op args[0]
  2.4 150.8 %shard_map.95 = (f32[54,128]{1,0:T(8,128)}, bf16[8192,384]{1,0:T(8,128)(2,1)}) custom-call(bf16[512,192]{1,0:T(8,128)(2,1)} %copy.10.trunk, bf16[8,192,384]{2,1,0:T(8,128)(2,1)} %bitcast.4, bf16[8192,384]{1,0:T(8,128)(2,1)} %base.1, bf16[2,1152,384]{2,1,0:T(8,128)(2,1)} %bitcast.3, bf16[7,384,768]{2,1,0:T(8,128)(2,1)} %headw.1, bf16[7,768]{1,0:T(8,128)(2,1)} %headl.1, ...), custom_call_target="tpu_custom_call" | custom-call | tf_op jit(solution)/shard_map/pallas_call | solution.py:371
  153.2 1.4 copy.13
  154.6 6.1 %copy.14 = bf16[8192,384]{1,0:T(8,128)(2,1)} copy(bf16[8192,384]{1,0:T(8,128)(2,1)} %get-tuple-element.5) | data formatting | bytes 12582912

commit v2 on v1

--- a/solution.py
+++ b/solution.py
@@ -264,12 +264,6 @@
     loads[3].wait()
     chosen[tp] = normalize(picked[...])
 
-    def drain(index, carry):
-        both(halo_copy(index, 1).wait_send, halo_copy(index, 0).wait_send)
-        return carry
-
-    lax.fori_loop(0, count, drain, 0)
-
     def chosen_copy(step):
         return remote(
             chosen.at[tp], chosen.at[tp], chosen_send.at[step - 1], chosen_recv.at[step - 1],
@@ -332,6 +326,12 @@
         trunk_copies[step - 1].wait_send()
     for copies in (raw_copies, proj_copies):
         both(copies[1].wait_send, copies[0].wait_send)
+
+    def drain(index, carry):
+        both(halo_copy(index, 1).wait_send, halo_copy(index, 0).wait_send)
+        return carry
+
+    lax.fori_loop(0, count, drain, 0)
 
     def drain_tower(index, carry):
         for part in range(2):

time: 161 us -> 161 us (level)
  no operation moved by 1% of the time
where the time goes in v2:
time: 161 us
  Pallas kernels  151 us (94%)
  local copies, waits for them, and re-layouts  9.24 us (6%)
    pallas_call x1, Pallas kernels, on_device(): pl.pallas_call(functools.partial(kernel, dims), out_shape=(jax.ShapeDtype...  151 us
    unnamed x3, local copies, waits for them, and re-layouts  9.24 us

profile of v2, /device:TPU:0, one launch (start us, length us, event | category | flops | bytes accessed | tf_op | source)
XLA Modules:
  0.0 160.5 jit_solution(9217824432890841813)
XLA Ops:
  0.6 1.8 %copy.10.trunk = bf16[512,192]{1,0:T(8,128)(2,1)} copy(bf16[512,192]{0,1:T(8,128)(2,1)} %param.8) | data formatting | bytes 393216 | tf_op args[0]
  2.4 150.6 %shard_map.95 = (f32[54,128]{1,0:T(8,128)}, bf16[8192,384]{1,0:T(8,128)(2,1)}) custom-call(bf16[512,192]{1,0:T(8,128)(2,1)} %copy.10.trunk, bf16[8,192,384]{2,1,0:T(8,128)(2,1)} %bitcast.4, bf16[8192,384]{1,0:T(8,128)(2,1)} %base.1, bf16[2,1152,384]{2,1,0:T(8,128)(2,1)} %bitcast.3, bf16[7,384,768]{2,1,0:T(8,128)(2,1)} %headw.1, bf16[7,768]{1,0:T(8,128)(2,1)} %headl.1, ...), custom_call_target="tpu_custom_call" | custom-call | tf_op jit(solution)/shard_map/pallas_call | solution.py:371
  153.0 1.4 copy.13
  154.4 6.1 %copy.14 = bf16[8192,384]{1,0:T(8,128)(2,1)} copy(bf16[8192,384]{1,0:T(8,128)(2,1)} %get-tuple-element.5) | data formatting | bytes 12582912
